TPU v7x, 256 devices: a whole 4x4x8 slice. The times are simulated.
256 devices in a mesh: expert: 32 (over y, x, core), group: 8 (over z).
Axes of the slice: x: 4, y: 4, z: 8, core: 2. Of those that a mesh axis runs over, the one named last changes fastest.
Arguments:
- activations: bfloat16 [4096, 7168], P('expert', 'group'), may hold values from -6 to 6
- out_grads: bfloat16 [4096, 7168], P('expert', 'group'), may hold values from -6 to 6
- sketch_op: bfloat16 [7168, 128], P('group'), may hold values from -0.0625 to 0.0625
- block_lists: int32 [256, 32], P('expert'), may hold values from 0 to 31, as said below
- block_counts: int32 [256], P('expert'), may hold values from 1 to 32
- gate_values: bfloat16 [256, 32, 128], P('expert'), may hold values from 0.05 to 9, as said below
Outputs:
- basis_out: float32 [256, 7168, 128], P('expert', 'group')
Inputs may be any that keep to these rules, and one draw needn't show every extreme that they name: `block_lists`: each row is an ordering of all 32 block numbers, each once. `gate_values`: positive.
All inputs are finite; a program needn't handle non-finite values.
Results may differ from a plain program's by a relative error of at most 0.0042.
The roundings to bfloat16 on the way count: a program that leaves them out, or rounds other values in their place, can miss the bound.
Values may be sent and summed in bfloat16 or wider, within the bound.
No kernel may reach another device: no remote copies, remote signals or barrier semaphores. Data moves between devices by JAX's collectives and lax.ppermute only.
A program may use at most 64 MiB of HBM per device.

v0:
```python
import math
import jax
import jax.numpy as jnp
from jax import lax
from jax.sharding import PartitionSpec as P


def sketch_rows(rows_x, rows_y, weight_part):
    count_exp = weight_part.shape[0]
    row_count = rows_x.shape[0]
    sketch_rank = rows_y.shape[1]
    rows_wide = rows_y.astype(jnp.float32)
    contract = (((0,), (0,)), ((), ()))
    scaled = (weight_part.T[:, :, None] * rows_wide[:, None, :]).astype(jnp.bfloat16)
    scaled = scaled.reshape(row_count, count_exp * sketch_rank)
    return lax.dot_general(rows_x, scaled, contract, preferred_element_type=jnp.float32)


def gram_of(sketch_flat, sketch_rank):
    shaped = sketch_flat.reshape(sketch_flat.shape[0], -1, sketch_rank)
    return jnp.einsum("dkr,dks->rs", shaped, shaped, precision=lax.Precision.HIGHEST)


def on_device(activations, out_grads, sketch_op, block_lists, block_counts, gate_values):
    sketch_rank = sketch_op.shape[1]
    feat_width = activations.shape[1]
    local_exp = block_lists.shape[0]
    blocks = block_lists.shape[1]
    partial_sketch = jnp.dot(out_grads, sketch_op, preferred_element_type=jnp.float32)
    sketched = lax.psum(partial_sketch, "group").astype(jnp.bfloat16)
    slot_ids = jnp.arange(blocks, dtype=jnp.int32)
    slot_live = slot_ids[None, :] < block_counts[:, None]
    onehot = ((block_lists[:, :, None] == slot_ids[None, None, :]) & slot_live[:, :, None]).astype(
        jnp.float32
    )
    weights = jnp.einsum("ejb,ejt->ebt", onehot, gate_values.astype(jnp.float32)).reshape(
        local_exp, -1
    )
    piece_rows = lax.all_gather(activations, "expert", axis=0, tiled=True)
    piece_sketch = lax.all_gather(sketched, "expert", axis=0, tiled=True)
    sketch_all = sketch_rows(piece_rows, piece_sketch, weights)
    gram_total = lax.psum(gram_of(sketch_all, sketch_rank), ("expert", "group"))
    factor = jnp.linalg.cholesky(gram_total)
    stacked = (
        sketch_all.reshape(feat_width, local_exp, sketch_rank)
        .transpose(1, 0, 2)
        .reshape(-1, sketch_rank)
    )
    basis_flat = lax.linalg.triangular_solve(
        factor, stacked, left_side=False, lower=True, transpose_a=True
    )
    out_scale = math.sqrt(local_exp * lax.axis_size("expert") * feat_width * lax.axis_size("group"))
    return (basis_flat * out_scale).reshape(local_exp, feat_width, sketch_rank)


def solution(mesh):
    in_specs = (
        P("expert", "group"),
        P("expert", "group"),
        P("group", None),
        P("expert", None),
        P("expert"),
        P("expert", None, None),
    )
    out_specs = P("expert", "group", None)
    return jax.shard_map(
        on_device, mesh=mesh, in_specs=in_specs, out_specs=out_specs, check_vma=False
    )
```

profile of v0, /device:TPU:1, one launch (start us, length us, event | category | flops | bytes accessed | tf_op | source)
XLA Modules:
  0.0 443.5 jit_solution(5734964180359648877)
XLA Ops:
  6.5 0.0 copy-start
  6.5 0.0 all-gather.3.cloned.1.call-start
  6.5 0.9 copy-done
  7.5 1.1 fusion.10
  8.6 27.5 %psum.14 = bf16[128,128]{1,0:T(8,128)(2,1)} all-reduce(f32[128,128]{1,0:T(8,128)S(1)} %fusion.10), channel_id=1, replica_groups=mesh['expert'=32,'group'=8] {'group'}, use_global_device_ids=true, to_apply=%region_0.0 | all-reduce | flops 16384 | bytes 98304 | tf_op jit(solution)/shard_map/psum | solution.py:30
  36.2 0.0 all-gather.3.cloned.1.call-update
  36.2 0.0 all-gather.5.cloned.1.call-start
  36.2 0.7 all-gather.5.cloned.1.call-update
  36.9 0.0 all-reduce.2.cloned.1.call-start
  37.0 0.7 iota_compare_fusion.3
  37.7 1.0 convolution_bitcast_fusion
  38.7 0.1 copy.26
  38.8 0.6 copy.11
  39.4 50.1 %all-gather.3.cloned.1.call-done = bf16[4096,128]{1,0:T(8,128)(2,1)} async-done(((bf16[128,128]{1,0:T(8,128)(2,1)}), bf16[4096,128]{1,0:T(8,128)(2,1)}) %all-gather.3.cloned.1.call-update) | async-done | bytes 1048592 | tf_op jit(solution)/shard_map/all_gather | solution.py:40
  89.5 1.4 convert_element_type.16
  90.9 16.4 %multiply_convert_fusion = bf16[4096,8,128]{2,1,0:T(8,128)(2,1)} fusion(f32[4096,128]{1,0:T(8,128)S(1)} %convert_element_type.16, f32[4096,8]{1,0:T(8,128)S(1)} %copy.11), kind=kLoop, calls=%fused_computation | loop fusion | flops 8388608 | bytes 10616832 | tf_op jit(solution)/shard_map/convert_element_type | solution.py:14
  107.2 40.0 %all-gather.5.cloned.1.call-done = bf16[4096,896]{1,0:T(8,128)(2,1)} async-done(((bf16[128,896]{1,0:T(8,128)(2,1)}), bf16[4096,896]{1,0:T(8,128)(2,1)}) %all-gather.5.cloned.1.call-update) | async-done | bytes 7340048 | tf_op jit(solution)/shard_map/all_gather | solution.py:39
  147.3 12.9 %fusion = f32[1024,896]{1,0:T(8,128)S(1)} fusion(bf16[4096,896]{1,0:T(8,128)(2,1)} %all-gather.5.cloned.1.call-done, bf16[512,8,8,128]{3,2,1,0:T(8,128)(2,1)} %bitcast.40), kind=kOutput, calls=%fused_computation.2 | convolution fusion | flops 7516192768 | bytes 19398656 | tf_op jit(solution)/shard_map/dot_general | solution.py:16
  160.2 0.0 copy-start.1
  160.2 1.8 copy-done.1
  162.1 3.6 convolution_bitcast_fusion.1
  165.7 0.0 all-reduce.2.cloned.1.call-update
  165.7 5.0 %copy.12 = f32[896,8,128]{2,0,1:T(8,128)} copy(f32[896,8,128]{0,2,1:T(8,128)} %bitcast.38) | data formatting | bytes 7340032 | tf_op jit(solution)/shard_map/reshape | solution.py:45
  170.7 235.7 %all-reduce.2.cloned.1.call-done = f32[128,128]{0,1:T(8,128)} async-done(((f32[128,128]{0,1:T(8,128)}), f32[128,128]{0,1:T(8,128)}) %all-reduce.2.cloned.1.call-update) | async-done | bytes 65552 | tf_op jit(solution)/shard_map/psum | solution.py:42
  406.4 0.9 copy.15
  407.4 0.9 fusion.7
  408.2 11.7 %cholesky.16 = f32[128,128]{1,0:T(8,128)S(1)} custom-call(f32[128,128]{1,0:T(8,128)S(1)} %fusion.7), custom_call_target="Cholesky" | custom-call | tf_op jit(solution)/shard_map/jit(cholesky)/cholesky | solution.py:43
  420.0 0.6 compare_reduce_fusion
  420.6 0.7 fusion.5
  421.3 9.8 %custom-call.6 = f32[1,128,128]{1,2,0:T(8,128)S(1)} custom-call(f32[1,128,128]{2,1,0:T(8,128)S(1)} %fusion.5), custom_call_target="InvertDiagBlocksLowerTriangular" | custom-call | tf_op jit(solution)/shard_map/triangular_solve | solution.py:49
  431.1 5.9 %convolution_multiply_fusion = f32[7168,128]{1,0:T(8,128)} fusion(f32[7168,128]{1,0:T(8,128)} %bitcast.39, f32[1,128,128]{1,2,0:T(8,128)S(1)} %custom-call.6), kind=kOutput, calls=%fused_computation.1 | convolution fusion | flops 1410203648 | bytes 7405568 | tf_op jit(solution)/shard_map/triangular_solve | solution.py:49
  (1 shorter events, 0.0 us)
Async XLA Ops:
  6.5 0.9 copy-start
  6.5 83.0 %all-gather.3.cloned.1.call-start = ((), (), s32[]{:S(2)}) async-start(), calls=%async_computation | async-start | bytes 1081344 | tf_op jit(solution)/shard_map/all_gather | solution.py:40
  36.2 111.1 %all-gather.5.cloned.1.call-start = ((), (), s32[]{:S(2)}) async-start(), calls=%async_computation.1 | async-start | bytes 7569408 | tf_op jit(solution)/shard_map/all_gather | solution.py:39
  36.9 369.5 %all-reduce.2.cloned.1.call-start = ((), (), s32[]{:S(2)}) async-start(), calls=%async_computation.2 | async-start | bytes 131072 | tf_op jit(solution)/shard_map/psum | solution.py:42
  160.2 1.8 copy-start.1
Sparse Core Ops, SparseCore 0:
  36.3 53.1 all-gather.2
  92.0 55.1 all-gather.4
  165.8 240.5 all-reduce.1
where the time goes:
time: 444 us
  waiting for transfers between devices  327 us (74%)
  other arithmetic  42.2 us (10%)
  blocking collectives  27.5 us (6%)
  matrix products  24.7 us (6%)
  between operations  13.2 us (3%)
  local copies, waits for them, and re-layouts  9.39 us (2%)
    psum x1, waiting for transfers between devices, on_device(): gram_total = lax.psum(gram_of(sketch_all, sketch_rank), ('expert', 'group'))  236 us
    all_gather x1, waiting for transfers between devices, on_device(): piece_sketch = lax.all_gather(sketched, 'expert', axis=0, tiled=True)  50.1 us
    all_gather x1, waiting for transfers between devices, on_device(): piece_rows = lax.all_gather(activations, 'expert', axis=0, tiled=True)  40 us
    psum x1, blocking collectives, on_device(): sketched = lax.psum(partial_sketch, 'group').astype(jnp.bfloat16)  27.5 us
    convert_element_type x1, other arithmetic, sketch_rows(): (weight_part.T[:, :, None] * rows_wide[:, None, :]).astype(jnp.bfloat16)  16.4 us
    dot_general x1, matrix products, sketch_rows(): lax.dot_general(rows_x, scaled, contract, preferred_element_type=jnp.floa...  12.9 us
    another operation x3, other arithmetic, on_device(): factor = jnp.linalg.cholesky(gram_total)  12.4 us
    another operation x2, other arithmetic, on_device(): lax.linalg.triangular_solve(factor, stacked, left_side=False, lower=True,...  10.5 us
  transfers between devices with their start and end apart: 3, of which 3 were waited for; matrix products, arithmetic and copies ran while one was open for 6% of the time, Pallas kernels for 0%

commit v1 on v0

--- a/solution.py
+++ b/solution.py
@@ -3,6 +3,7 @@
 import jax.numpy as jnp
 from jax import lax
 from jax.sharding import PartitionSpec as P
+from jax.lax import all_gather
 
 
 def sketch_rows(rows_x, rows_y, weight_part):
@@ -39,7 +40,8 @@
     piece_rows = lax.all_gather(activations, "expert", axis=0, tiled=True)
     piece_sketch = lax.all_gather(sketched, "expert", axis=0, tiled=True)
     sketch_all = sketch_rows(piece_rows, piece_sketch, weights)
-    gram_total = lax.psum(gram_of(sketch_all, sketch_rank), ("expert", "group"))
+    my_tile = gram_of(sketch_all, sketch_rank)
+    gram_total = jnp.sum(all_gather(my_tile, ("expert", "group")), 0)
     factor = jnp.linalg.cholesky(gram_total)
     stacked = (
         sketch_all.reshape(feat_width, local_exp, sketch_rank)

time: 444 us -> 333 us (0.75)
  waiting for transfers between devices: 327 us -> 210 us
  other arithmetic: 42.2 us -> 47.9 us
    psum x1 -> x0, waiting for transfers between devices: 236 us -> none  [on_device(): gram_total = lax.psum(gram_of(sketch_all, sketch_rank), ('expert', 'group'))]
    all_gather x0 -> x1, waiting for transfers between devices: none -> 120 us  [on_device(): gram_total = jnp.sum(all_gather(my_tile, ('expert', 'group')), 0)]
    reduce_sum x0 -> x1, other arithmetic: none -> 6.59 us  [on_device(): gram_total = jnp.sum(all_gather(my_tile, ('expert', 'group')), 0)]
  transfers between devices with their start and end apart: 3 -> 3, of which waited for: 3 -> 3; matrix products, arithmetic and copies ran while one was open for 6% -> 8% of each run, Pallas kernels for 0% -> 0%
where the time goes in v1:
time: 333 us; the launch traced here: 332 us
  waiting for transfers between devices  210 us (63%)
  other arithmetic  47.9 us (14%)
  blocking collectives  27.5 us (8%)
  matrix products  24.6 us (7%)
  between operations  13.2 us (4%)
  local copies, waits for them, and re-layouts  8.55 us (3%)
    all_gather x1, waiting for transfers between devices, on_device(): gram_total = jnp.sum(all_gather(my_tile, ('expert', 'group')), 0)  120 us
    all_gather x1, waiting for transfers between devices, on_device(): piece_sketch = lax.all_gather(sketched, 'expert', axis=0, tiled=True)  50.1 us
    all_gather x1, waiting for transfers between devices, on_device(): piece_rows = lax.all_gather(activations, 'expert', axis=0, tiled=True)  40 us
    psum x1, blocking collectives, on_device(): sketched = lax.psum(partial_sketch, 'group').astype(jnp.bfloat16)  27.5 us
    convert_element_type x1, other arithmetic, sketch_rows(): (weight_part.T[:, :, None] * rows_wide[:, None, :]).astype(jnp.bfloat16)  16.4 us
    dot_general x1, matrix products, sketch_rows(): lax.dot_general(rows_x, scaled, contract, preferred_element_type=jnp.floa...  12.9 us
    another operation x3, other arithmetic, on_device(): factor = jnp.linalg.cholesky(gram_total)  12.4 us
    another operation x2, other arithmetic, on_device(): lax.linalg.triangular_solve(factor, stacked, left_side=False, lower=True,...  10.5 us
  transfers between devices with their start and end apart: 3, of which 3 were waited for; matrix products, arithmetic and copies ran while one was open for 8% of the time, Pallas kernels for 0%

profile of v1, /device:TPU:1, one launch (start us, length us, event | category | flops | bytes accessed | tf_op | source)
XLA Modules:
  0.0 332.3 jit_solution(6978671600779309800)
XLA Ops:
  6.5 0.0 copy-start
  6.5 0.0 all-gather.5.cloned.1.call-start
  6.5 0.9 copy-done
  7.5 1.1 fusion.10
  8.6 27.5 %psum.7 = bf16[128,128]{1,0:T(8,128)(2,1)} all-reduce(f32[128,128]{1,0:T(8,128)S(1)} %fusion.10), channel_id=1, replica_groups=mesh['expert'=32,'group'=8] {'group'}, use_global_device_ids=true, to_apply=%region_0.0 | all-reduce | flops 16384 | bytes 98304 | tf_op jit(solution)/shard_map/psum | solution.py:31
  36.2 0.0 all-gather.5.cloned.1.call-update
  36.2 0.0 all-gather.7.cloned.1.call-start
  36.2 0.7 all-gather.7.cloned.1.call-update
  36.9 0.0 all-gather.9.cloned.1.call-start
  37.0 0.7 iota_compare_fusion.3
  37.7 1.0 convolution_bitcast_fusion
  38.7 0.1 copy.26
  38.8 0.6 copy.14
  39.4 50.1 %all-gather.5.cloned.1.call-done = bf16[4096,128]{1,0:T(8,128)(2,1)} async-done(((bf16[128,128]{1,0:T(8,128)(2,1)}), bf16[4096,128]{1,0:T(8,128)(2,1)}) %all-gather.5.cloned.1.call-update) | async-done | bytes 1048592 | tf_op jit(solution)/shard_map/all_gather | solution.py:41
  89.5 1.4 convert_element_type.16
  90.9 16.4 %multiply_convert_fusion = bf16[4096,8,128]{2,1,0:T(8,128)(2,1)} fusion(f32[4096,128]{1,0:T(8,128)S(1)} %convert_element_type.16, f32[4096,8]{1,0:T(8,128)S(1)} %copy.14), kind=kLoop, calls=%fused_computation | loop fusion | flops 8388608 | bytes 10616832 | tf_op jit(solution)/shard_map/convert_element_type | solution.py:15
  107.2 40.0 %all-gather.7.cloned.1.call-done = bf16[4096,896]{1,0:T(8,128)(2,1)} async-done(((bf16[128,896]{1,0:T(8,128)(2,1)}), bf16[4096,896]{1,0:T(8,128)(2,1)}) %all-gather.7.cloned.1.call-update) | async-done | bytes 7340048 | tf_op jit(solution)/shard_map/all_gather | solution.py:40
  147.3 12.9 %fusion = f32[1024,896]{1,0:T(8,128)S(1)} fusion(bf16[4096,896]{1,0:T(8,128)(2,1)} %all-gather.7.cloned.1.call-done, bf16[512,8,8,128]{3,2,1,0:T(8,128)(2,1)} %bitcast.42), kind=kOutput, calls=%fused_computation.2 | convolution fusion | flops 7516192768 | bytes 19398656 | tf_op jit(solution)/shard_map/dot_general | solution.py:17
  160.2 0.0 copy-start.1
  160.2 1.8 copy-done.1
  162.1 3.6 %convolution_bitcast_fusion.1 = f32[128,128]{1,0:T(8,128)} fusion(f32[896,8,128]{0,2,1:T(8,128)S(1)} %bitcast.38), kind=kOutput, calls=%fused_computation.6 | convolution fusion | flops 1409286144 | bytes 3735552 | tf_op jit(solution)/shard_map/dkr,dks->rs/dot_general | solution.py:22
  165.7 0.0 all-gather.9.cloned.1.call-update
  165.7 5.0 %copy.15 = f32[896,8,128]{2,0,1:T(8,128)} copy(f32[896,8,128]{0,2,1:T(8,128)} %bitcast.39) | data formatting | bytes 7340032 | tf_op jit(solution)/shard_map/reshape | solution.py:47
  170.7 119.5 %all-gather.9.cloned.1.call-done = f32[32768,128]{1,0:T(8,128)} async-done(((f32[128,128]{1,0:T(8,128)}), f32[32768,128]{1,0:T(8,128)}) %all-gather.9.cloned.1.call-update) | async-done | bytes 16777232 | tf_op jit(solution)/shard_map/all_gather | solution.py:44
  290.3 6.6 %reduce_sum.9 = f32[128,128]{1,0:T(8,128)S(1)} reduce(f32[256,128,128]{2,1,0:T(8,128)} %bitcast.40, f32[]{:T(128)} %constant.39.clone.1), dimensions={0}, to_apply=%region_1.0 | reduce | flops 4177920 | bytes 16842756 | tf_op jit(solution)/shard_map/reduce_sum | solution.py:44
  296.8 0.1 copy.17
  297.0 11.7 %cholesky.16 = f32[128,128]{1,0:T(8,128)S(1)} custom-call(f32[128,128]{1,0:T(8,128)S(1)} %fusion.7), custom_call_target="Cholesky" | custom-call | tf_op jit(solution)/shard_map/jit(cholesky)/cholesky | solution.py:45
  308.7 0.6 compare_reduce_fusion
  309.3 0.7 fusion.5
  310.0 9.8 %custom-call.6 = f32[1,128,128]{1,2,0:T(8,128)S(1)} custom-call(f32[1,128,128]{2,1,0:T(8,128)S(1)} %fusion.5), custom_call_target="InvertDiagBlocksLowerTriangular" | custom-call | tf_op jit(solution)/shard_map/triangular_solve | solution.py:51
  319.8 5.9 %convolution_multiply_fusion = f32[7168,128]{1,0:T(8,128)} fusion(f32[7168,128]{1,0:T(8,128)} %bitcast.41, f32[1,128,128]{1,2,0:T(8,128)S(1)} %custom-call.6), kind=kOutput, calls=%fused_computation.1 | convolution fusion | flops 1410203648 | bytes 7405568 | tf_op jit(solution)/shard_map/triangular_solve | solution.py:51
  (2 shorter events, 0.0 us)
Async XLA Ops:
  6.5 0.9 copy-start
  6.5 83.0 %all-gather.5.cloned.1.call-start = ((), (), s32[]{:S(2)}) async-start(), calls=%async_computation | async-start | bytes 1081344 | tf_op jit(solution)/shard_map/all_gather | solution.py:41
  36.2 111.1 %all-gather.7.cloned.1.call-start = ((), (), s32[]{:S(2)}) async-start(), calls=%async_computation.1 | async-start | bytes 7569408 | tf_op jit(solution)/shard_map/all_gather | solution.py:40
  36.9 253.3 %all-gather.9.cloned.1.call-start = ((), (), s32[]{:S(2)}) async-start(), calls=%async_computation.2 | async-start | bytes 16842752 | tf_op jit(solution)/shard_map/all_gather | solution.py:44
  160.2 1.8 copy-start.1
Sparse Core Ops, SparseCore 0:
  36.3 53.1 all-gather.4
  92.0 55.1 all-gather.6
  165.8 124.3 all-gather.8
